TPU v7x, 32 devices: a whole 2x2x4 slice. The times are simulated.
32 devices in a mesh: slab: 8 (over y, x, core), group: 4 (over z).
Axes of the slice: x: 2, y: 2, z: 4, core: 2. Of those that a mesh axis runs over, the one named last changes fastest.
Arguments:
- disp_now: float32 [3, 262144], P(None, 'slab'), may hold values from -6 to 6
- disp_prev: float32 [3, 262144], P(None, 'slab'), may hold values from -6 to 6
- inv_mass: float32 [262144], P('slab'), may hold values from 0.5 to 2
- cell_nodes: int32 [1024, 192], P(('slab', 'group')), may hold values from 0 to 98303
- shape_grads: bfloat16 [1024, 3, 192, 128], P(('slab', 'group')), may hold values from -0.125 to 0.125
- cell_weights: float32 [1024, 128], P(('slab', 'group')), may hold values from 0.5 to 2
- cell_shear: float32 [1024], P(('slab', 'group')), may hold values from 0.5 to 2
- cell_bulk: float32 [1024], P(('slab', 'group')), may hold values from 1 to 4
- block_owner: int32 [1024, 1], P(('slab', 'group')), may hold values from 0 to 7; in each aligned block of 32 rows (0 to 31, 32 to 63, ...) at most 4 rows name the same one
- block_nodes: int32 [1024, 256], P(('slab', 'group')), may hold values from 0 to 32767
- block_phi: float32 [1024, 128, 256], P(('slab', 'group')), may hold values from -0.375 to 0.375
- block_corr: float32 [1024, 128, 128], P(('slab', 'group')), may hold values from -0.5 to 0.5
- block_target: float32 [1024, 3, 128], P(('slab', 'group')), may hold values from -6 to 6
- block_fixed: int32 [1024, 128], P(('slab', 'group')), may hold values 0 or 1
Outputs:
- disp_final: float32 [3, 262144], P(None, 'slab')
Inputs may be any that keep to these rules, and one draw needn't show every extreme that they name: `cell_nodes`: support node numbers run over the slab below, the cell's own slab and the slab above; those outside the head read zero. `block_owner`: among the 32 blocks of one device at most 4 have one owner slab, and in every draw some device has exactly 4 with one owner.
All inputs are finite; a program needn't handle non-finite values. No bound on the sum of `block_fixed` on one device may be relied on, other than what follows from the above.
Results may differ from a plain program's by a relative error of at most 0.0059.
Values may be sent and summed in bfloat16 or wider, within the bound.
No kernel may reach another device: no remote copies, remote signals or barrier semaphores. Data moves between devices by JAX's collectives and lax.ppermute only.
A program may use at most 192 MiB of HBM per device.

v0:
```python
import jax
import jax.numpy as jnp
from jax import lax
from jax.sharding import PartitionSpec as P

CAP = 4


def extended(block, sides, width):
    for axis, dim in sides:
        count = lax.axis_size(axis)
        forward = [(i, i + 1) for i in range(count - 1)]
        backward = [(target, source) for source, target in forward]
        low = lax.ppermute(
            lax.slice_in_dim(block, block.shape[dim] - width, None, axis=dim), axis, forward
        )
        high = lax.ppermute(lax.slice_in_dim(block, 0, width, axis=dim), axis, backward)
        block = jnp.concatenate([low, block, high], axis=dim)
    return block


def from_behind(array, axis, by):
    size = lax.axis_size(axis)
    pairs = [(i, i + by) for i in range(size) if 0 <= i + by < size]
    return lax.ppermute(array, axis, pairs)


def stress_of(grad, shear, bulk):
    identity = jnp.eye(3, dtype=grad.dtype)
    full = grad + identity[None, :, :, None]
    entries = [[full[:, leading, trailing] for trailing in range(3)] for leading in range(3)]
    cofactor = [
        [
            entries[(leading + 1) % 3][(trailing + 1) % 3]
            * entries[(leading + 2) % 3][(trailing + 2) % 3]
            - entries[(leading + 1) % 3][(trailing + 2) % 3]
            * entries[(leading + 2) % 3][(trailing + 1) % 3]
            for trailing in range(3)
        ]
        for leading in range(3)
    ]
    volume = (
        entries[0][0] * cofactor[0][0]
        + entries[0][1] * cofactor[0][1]
        + entries[0][2] * cofactor[0][2]
    )
    clamped = jnp.maximum(volume, 0.3)
    shear_now = shear[:, None]
    factor = (bulk[:, None] * jnp.log(clamped) - shear_now) / clamped
    rows_out = [
        jnp.stack(
            [
                shear_now * entries[leading][trailing] + factor * cofactor[leading][trailing]
                for trailing in range(3)
            ],
            axis=1,
        )
        for leading in range(3)
    ]
    return jnp.stack(rows_out, axis=1)


def body(
    disp_now,
    disp_prev,
    inv_mass,
    cell_nodes,
    shape_grads,
    cell_weights,
    cell_shear,
    cell_bulk,
    block_owner,
    block_nodes,
    block_phi,
    block_corr,
    block_target,
    block_fixed,
):
    width = disp_now.shape[1]
    slabs = lax.axis_size("slab")
    nearby = extended(disp_now.astype(jnp.bfloat16), (("slab", 1),), width)
    gathered = jnp.moveaxis(jnp.take(nearby, cell_nodes, axis=1), 0, 1)
    grad = jnp.einsum("cia,cjap->cijp", gathered, shape_grads, preferred_element_type=jnp.float32)
    stress = stress_of(grad, cell_shear, cell_bulk)
    weighted = (cell_weights[:, None, None, :] * stress).astype(jnp.bfloat16)
    force = jnp.einsum("cijp,cjap->cia", weighted, shape_grads, preferred_element_type=jnp.float32)
    partial_value = (
        jnp.zeros((3, 3 * width), jnp.float32).at[:, cell_nodes].add(jnp.moveaxis(force, 1, 0))
    )
    summed = lax.psum(partial_value, "group")
    from_above = from_behind(summed[:, :width], "slab", -1)
    from_below = from_behind(summed[:, 2 * width :], "slab", 1)
    force_sum = summed[:, width : 2 * width] + from_above + from_below
    disp_next = 2.0 * disp_now - disp_prev - inv_mass[None, :] * force_sum
    support = block_nodes.shape[1]
    owner = block_owner[:, 0]
    matches = (owner[:, None] == jnp.arange(slabs, dtype=jnp.int32)[None, :]).astype(jnp.int32)
    ranked = jnp.sum((jnp.cumsum(matches, axis=0) - matches) * matches, axis=1)
    slot_of = owner * CAP + ranked
    fixed_mask = block_fixed.astype(jnp.float32)
    highest = lax.Precision.HIGHEST
    request = jnp.zeros((slabs * CAP, support), jnp.int32).at[slot_of].set(block_nodes)
    request = request.reshape(slabs, CAP, support)
    asked = lax.all_to_all(request, "slab", split_axis=0, concat_axis=0, tiled=True)
    looked = jnp.moveaxis(jnp.take(disp_next, asked, axis=1), 0, 2)
    returned = lax.all_to_all(looked, "slab", split_axis=0, concat_axis=0, tiled=True)
    returned, asked = (returned, asked)
    values = returned.reshape(slabs * CAP, 3, support)[slot_of]
    interp = jnp.einsum("bma,bia->bim", block_phi, values, precision=highest)
    resid = fixed_mask[:, None, :] * (block_target - interp)
    corr = jnp.einsum("bmq,biq->bim", block_corr, resid, precision=highest)
    delta = jnp.einsum("bma,bim->bia", block_phi, corr, precision=highest)
    outgoing = jnp.zeros((slabs * CAP, 3, support), jnp.float32).at[slot_of].set(delta)
    arrived = lax.all_to_all(
        outgoing.reshape(slabs, CAP, 3, support), "slab", split_axis=0, concat_axis=0, tiled=True
    )
    added = jnp.zeros((3, width), jnp.float32).at[:, asked].add(jnp.moveaxis(arrived, 2, 0))
    return disp_next + lax.psum(added, "group")


def solution(mesh):
    placed = (
        P(None, "slab"),
        P(None, "slab"),
        P("slab"),
        P(("slab", "group"), None),
        P(("slab", "group"), None, None, None),
        P(("slab", "group"), None),
        P(("slab", "group")),
        P(("slab", "group")),
        P(("slab", "group"), None),
        P(("slab", "group"), None),
        P(("slab", "group"), None, None),
        P(("slab", "group"), None, None),
        P(("slab", "group"), None, None),
        P(("slab", "group"), None),
    )
    return jax.shard_map(
        body, mesh=mesh, in_specs=placed, out_specs=P(None, "slab"), check_vma=False
    )
```

profile of v0, /device:TPU:0, one launch (start us, length us, event | category | flops | bytes accessed | tf_op | source)
XLA Modules:
  0.0 435.3 jit_solution(6011149501604761152)
XLA Ops:
  7.8 2.4 collective-permute-start
  13.2 2.7 collective-permute-done.1
  17.2 15.8 %copy.131 = bf16[3,98304]{0,1:T(8,128)(2,1)} copy(bf16[3,98304]{1,0:T(4,128)(2,1)S(1)} %pad_maximum_fusion) | data formatting | bytes 1179648 | tf_op jit(solution)/shard_map/concatenate | solution.py:18
  33.0 32.5 %gather_fusion = bf16[6144,3]{1,0:T(8,128)(2,1)} fusion(bf16[3,98304]{0,1:T(8,128)(2,1)} %copy.131, s32[6144]{0:T(1024)S(1)} %broadcast_clamp_fusion.1), kind=kCustom, calls=%fused_computation | custom fusion | bytes 98304 | tf_op jit(solution)/shard_map/jit(_take)/gather | solution.py:82
  65.5 1.9 copy.132
  67.5 3.3 fusion.10
  71.1 4.1 convolution_bitcast_fusion
  75.2 2.2 copy.149
  77.4 53.3 %scatter_custom_fusion = f32[3,98304]{0,1:T(8,128)} fusion(s32[6144]{0:T(1024)S(1)} %reshape.1417, f32[6144,3]{1,0:T(8,128)} %bitcast.170, f32[]{:T(128)} %constant.16.clone.1), kind=kCustom, calls=%fused_computation.7 | custom fusion | flops 18432 | bytes 1180160 | tf_op jit(solution)/shard_map/scatter-add | solution.py:88
  130.7 26.7 %copy.137 = f32[3,98304]{1,0:T(4,128)} copy(f32[3,98304]{0,1:T(8,128)} %scatter_custom_fusion) | data formatting | bytes 2359296 | tf_op jit(solution)/shard_map/scatter-add | solution.py:88
  159.3 8.0 %all-to-all-start = ((s32[8,4,256]{2,1,0:T(4,128)}), s32[8,4,256]{2,1,0:T(4,128)S(1)}, u32[]{:S(2)}, u32[]{:S(2)}) async-start(s32[8,4,256]{2,1,0:T(4,128)} %reshape.1388), calls=%async_computation | async-start | bytes 65536 | tf_op jit(solution)/shard_map/all_to_all | solution.py:104
  167.3 4.8 %all-to-all-done = s32[8,4,256]{2,1,0:T(4,128)S(1)} async-done(((s32[8,4,256]{2,1,0:T(4,128)}), s32[8,4,256]{2,1,0:T(4,128)S(1)}, u32[]{:S(2)}, u32[]{:S(2)}) %all-to-all-start) | async-done | bytes 32800 | tf_op jit(solution)/shard_map/all_to_all | solution.py:104
  172.2 59.9 %all-reduce.3.cloned.1.call-done = f32[3,98304]{1,0:T(4,128)} async-done(((f32[3,98304]{1,0:T(4,128)}), f32[3,98304]{1,0:T(4,128)}) %all-reduce.3.cloned.1.call-update) | async-done | bytes 1179664 | tf_op jit(solution)/shard_map/psum | solution.py:90
  232.1 1.4 fusion.22
  234.8 3.1 collective-permute-start.3
  237.9 1.4 collective-permute-done.3
  239.4 1.6 fusion.7
  240.9 8.6 %copy.138 = f32[3,32768]{0,1:T(8,128)} copy(f32[3,32768]{1,0:T(4,128)S(1)} %fusion.7) | data formatting | bytes 786432 | tf_op jit(solution)/shard_map/sub | solution.py:94
  249.5 33.5 %gather_fusion.1 = f32[8192,3]{1,0:T(8,128)} fusion(f32[3,32768]{0,1:T(8,128)} %copy.138, s32[8192]{0:T(1024)S(1)} %broadcast_clamp_fusion), kind=kCustom, calls=%fused_computation.1 | custom fusion | bytes 229376 | tf_op jit(solution)/shard_map/jit(_take)/gather | solution.py:105
  283.0 2.8 copy.139
  286.5 13.2 %all-to-all-start.1 = ((f32[8,4,3,256]{3,1,2,0:T(4,128)}), f32[8,4,3,256]{3,1,2,0:T(4,128)S(1)}, u32[]{:S(2)}, u32[]{:S(2)}) async-start(f32[8,4,3,256]{3,1,2,0:T(4,128)} %select_bitcast_fusion), calls=%async_computation.1 | async-start | bytes 196608 | tf_op jit(solution)/shard_map/all_to_all | solution.py:106
  299.7 5.1 %all-to-all-done.1 = f32[8,4,3,256]{3,1,2,0:T(4,128)S(1)} async-done(((f32[8,4,3,256]{3,1,2,0:T(4,128)}), f32[8,4,3,256]{3,1,2,0:T(4,128)S(1)}, u32[]{:S(2)}, u32[]{:S(2)}) %all-to-all-start.1) | async-done | bytes 98336 | tf_op jit(solution)/shard_map/all_to_all | solution.py:106
  305.5 5.8 %fusion.4 = f32[32,3,128]{2,1,0:T(4,128)S(1)} fusion(f32[32,3,256]{2,1,0:T(4,128)S(1)} %gather_fusion.2, f32[32,128,256]{2,1,0:T(8,128)} %param.24, f32[32,3,128]{2,0,1:T(8,128)S(1)} %copy-done.4, f32[32,128]{1,0:T(8,128)S(1)} %convert_element_type.23), kind=kOutput, calls=%fused_computation.13 | convolution fusion | flops 37773312 | bytes 4407296 | tf_op jit(solution)/shard_map/bma,bia->bim/dot_general | solution.py:109
  311.4 3.4 fusion.23
  314.7 2.1 fusion.24
  316.9 1.5 scatter_fusion
  318.4 7.6 %all_to_all.15 = f32[8,4,3,256]{3,1,2,0:T(4,128)S(1)} all-to-all(f32[8,4,3,256]{3,1,2,0:T(4,128)S(1)} %copy.143), channel_id=1, replica_groups=mesh['slab'=8,'group'=4] {'slab'}, dimensions={0} | all-to-all | bytes 196608 | tf_op jit(solution)/shard_map/all_to_all | solution.py:114
  326.0 2.6 copy.151
  328.6 51.1 %scatter_custom_fusion.3 = f32[3,32768]{0,1:T(8,128)} fusion(s32[8192]{0:T(1024)S(1)} %bitcast.176, f32[8192,3]{1,0:T(8,128)} %bitcast.169, f32[]{:T(128)} %constant.16.clone.1), kind=kCustom, calls=%fused_computation.9 | custom fusion | flops 24576 | bytes 393728 | tf_op jit(solution)/shard_map/scatter-add | solution.py:117
  379.7 9.8 %copy.146 = f32[3,32768]{1,0:T(4,128)} copy(f32[3,32768]{0,1:T(8,128)} %scatter_custom_fusion.3) | data formatting | bytes 786432 | tf_op jit(solution)/shard_map/scatter-add | solution.py:117
  389.5 37.0 %all-reduce.5.cloned.1.call-done = f32[3,32768]{1,0:T(4,128)} async-done(((f32[3,32768]{1,0:T(4,128)}), f32[3,32768]{1,0:T(4,128)}) %all-reduce.5.cloned.1.call-update) | async-done | bytes 393232 | tf_op jit(solution)/shard_map/psum | solution.py:118
  426.5 2.0 add.250
  (59 shorter events, 10.6 us)
Async XLA Ops:
  6.5 304.8 %copy-start = (f32[32,128,128]{2,1,0:T(8,128)S(1)}, f32[32,128,128]{2,1,0:T(8,128)}, u32[]{:S(2)}) copy-start(f32[32,128,128]{2,1,0:T(8,128)} %param.25) | copy-start | bytes 6291460
  6.5 225.6 %all-reduce.3.cloned.1.call-start = ((), (), s32[]{:S(2)}) async-start(), calls=%async_computation.3 | async-start | bytes 3145728 | tf_op jit(solution)/shard_map/psum | solution.py:90
  7.8 5.4 %collective-permute-start = (bf16[3,32768]{1,0:T(4,128)(2,1)S(1)}, bf16[3,32768]{1,0:T(4,128)(2,1)S(1)}, u32[]{:S(2)}, u32[]{:S(2)}) collective-permute-start(bf16[3,32768]{1,0:T(4,128)(2,1)S(1)} %convert_element_type.19), channel_id=1, source_target_pairs={{0,4},{4,8},{8,12},{12,16},{16,20},{20,24},{24,28},{1,5},{5,9},{9,... | collective-permute-start | bytes 589832 | tf_op jit(solution)/shard_map/ppermute | solution.py:14
  10.2 5.6 %collective-permute-start.1 = (bf16[3,32768]{1,0:T(4,128)(2,1)S(1)}, bf16[3,32768]{1,0:T(4,128)(2,1)}, u32[]{:S(2)}, u32[]{:S(2)}) collective-permute-start(bf16[3,32768]{1,0:T(4,128)(2,1)S(1)} %convert_element_type.19), channel_id=1, source_target_pairs={{4,0},{8,4},{12,8},{16,12},{20,16},{24,20},{28,24},{5,1},{9,5},{13... | collective-permute-start | bytes 589832 | tf_op jit(solution)/shard_map/ppermute | solution.py:17
  33.0 37.8 %copy-start.7 = (f32[32]{0:T(128)S(1)}, f32[32]{0:T(128)}, u32[]{:S(2)}) copy-start(f32[32]{0:T(128)} %param.20) | copy-start | bytes 388
  33.0 37.8 %copy-start.9 = (f32[32]{0:T(128)S(1)}, f32[32]{0:T(128)}, u32[]{:S(2)}) copy-start(f32[32]{0:T(128)} %param.21) | copy-start | bytes 388
  33.0 38.1 %copy-start.6 = (f32[32,128]{1,0:T(8,128)S(1)}, f32[32,128]{1,0:T(8,128)}, u32[]{:S(2)}) copy-start(f32[32,128]{1,0:T(8,128)} %param.19) | copy-start | bytes 49156
  130.7 26.7 %copy-start.8 = (s32[32,1]{0,1:T(1,128)S(1)}, s32[32,1]{0,1:T(1,128)}, u32[]{:S(2)}) copy-start(s32[32,1]{0,1:T(1,128)} %param.22) | copy-start | bytes 388
  130.7 36.6 %copy-start.5 = (s32[32,128]{1,0:T(8,128)S(1)}, s32[32,128]{1,0:T(8,128)}, u32[]{:S(2)}) copy-start(s32[32,128]{1,0:T(8,128)} %param.27) | copy-start | bytes 49156
  157.4 82.0 %copy-start.2 = (f32[3,32768]{1,0:T(4,128)S(1)}, f32[3,32768]{1,0:T(4,128)}, u32[]{:S(2)}) copy-start(f32[3,32768]{1,0:T(4,128)} %param.14) | copy-start | bytes 1179652
  157.4 82.0 %copy-start.3 = (f32[32768]{0:T(1024)S(1)}, f32[32768]{0:T(1024)}, u32[]{:S(2)}) copy-start(f32[32768]{0:T(1024)} %param.16) | copy-start | bytes 393220
  159.3 12.8 %all-to-all-start = ((s32[8,4,256]{2,1,0:T(4,128)}), s32[8,4,256]{2,1,0:T(4,128)S(1)}, u32[]{:S(2)}, u32[]{:S(2)}) async-start(s32[8,4,256]{2,1,0:T(4,128)} %reshape.1388), calls=%async_computation | async-start | bytes 65536 | tf_op jit(solution)/shard_map/all_to_all | solution.py:104
  233.5 4.4 %collective-permute-start.2 = (f32[3,32768]{1,0:T(4,128)S(1)}, f32[3,32768]{1,0:T(4,128)S(1)}, u32[]{:S(2)}, u32[]{:S(2)}) collective-permute-start(f32[3,32768]{1,0:T(4,128)S(1)} %get-tuple-element.9), channel_id=1, source_target_pairs={{4,0},{8,4},{12,8},{16,12},{20,16},{24,20},{28,24},{5,1},{9,5},{13... | collective-permute-start | bytes 1179656 | tf_op jit(solution)/shard_map/ppermute | solution.py:25
  234.8 4.6 %collective-permute-start.3 = (f32[3,32768]{1,0:T(4,128)S(1)}, f32[3,32768]{1,0:T(4,128)S(1)}, u32[]{:S(2)}, u32[]{:S(2)}) collective-permute-start(f32[3,32768]{1,0:T(4,128)S(1)} %get-tuple-element.10), channel_id=1, source_target_pairs={{0,4},{4,8},{8,12},{12,16},{16,20},{20,24},{24,28},{1,5},{5,9},{9,... | collective-permute-start | bytes 1179656 | tf_op jit(solution)/shard_map/ppermute | solution.py:25
  249.5 56.0 %copy-start.4 = (f32[32,3,128]{2,0,1:T(8,128)S(1)}, f32[32,3,128]{2,0,1:T(8,128)}, u32[]{:S(2)}) copy-start(f32[32,3,128]{2,0,1:T(8,128)} %param.26) | copy-start | bytes 147460
  286.5 18.4 %all-to-all-start.1 = ((f32[8,4,3,256]{3,1,2,0:T(4,128)}), f32[8,4,3,256]{3,1,2,0:T(4,128)S(1)}, u32[]{:S(2)}, u32[]{:S(2)}) async-start(f32[8,4,3,256]{3,1,2,0:T(4,128)} %select_bitcast_fusion), calls=%async_computation.1 | async-start | bytes 196608 | tf_op jit(solution)/shard_map/all_to_all | solution.py:106
  299.6 126.9 %all-reduce.5.cloned.1.call-start = ((), (), s32[]{:S(2)}) async-start(), calls=%async_computation.4 | async-start | bytes 1048576 | tf_op jit(solution)/shard_map/psum | solution.py:118
  305.5 9.2 %copy-start.1 = (f32[32,128,256]{2,1,0:T(8,128)S(1)}, f32[32,128,256]{2,1,0:T(8,128)}, u32[]{:S(2)}) copy-start(f32[32,128,256]{2,1,0:T(8,128)} %param.24) | copy-start | bytes 12582916
Sparse Core Ops, SparseCore 0:
  157.5 74.5 all-reduce.2
  389.6 36.8 all-reduce.4
where the time goes:
time: 437 us; the launch traced here: 435 us
  local copies, waits for them, and re-layouts  142 us (32%)
  other arithmetic  113 us (26%)
  waiting for transfers between devices  111 us (25%)
  starting transfers between devices  29.3 us (7%)
  matrix products  18.6 us (4%)
  between operations  13.7 us (3%)
  blocking collectives  7.58 us (2%)
    psum x1, waiting for transfers between devices, body(): summed = lax.psum(partial_value, 'group')  59.9 us
    scatter-add x1, other arithmetic, body(): jnp.zeros((3, 3 * width), jnp.float32).at[:, cell_nodes]  53.3 us
    scatter-add x1, other arithmetic, body(): jnp.zeros((3, width), jnp.float32).at[:, asked]  51.1 us
    psum x1, waiting for transfers between devices, body(): return disp_next + lax.psum(added, 'group')  37 us
    gather x2, local copies, waits for them, and re-layouts, body(): looked = jnp.moveaxis(jnp.take(disp_next, asked, axis=1), 0, 2)  36.3 us
    gather x2, local copies, waits for them, and re-layouts, body(): gathered = jnp.moveaxis(jnp.take(nearby, cell_nodes, axis=1), 0, 1)  34.5 us
    scatter-add x1, local copies, waits for them, and re-layouts, body(): jnp.zeros((3, 3 * width), jnp.float32).at[:, cell_nodes]  26.7 us
    concatenate x1, local copies, waits for them, and re-layouts, extended(): block = jnp.concatenate([low, block, high], axis=dim)  15.8 us
  transfers between devices with their start and end apart: 8, of which 6 were waited for; matrix products, arithmetic and copies ran while one was open for 1% of the time, Pallas kernels for 0%

commit v1 on v0

--- a/solution.py
+++ b/solution.py
@@ -87,7 +87,9 @@
     partial_value = (
         jnp.zeros((3, 3 * width), jnp.float32).at[:, cell_nodes].add(jnp.moveaxis(force, 1, 0))
     )
-    summed = lax.psum(partial_value, "group")
+    summed = partial_value
+    for hop in (1, 2):
+        summed = summed + lax.ppermute(summed, "group", [(dev, dev ^ hop) for dev in range(4)])
     from_above = from_behind(summed[:, :width], "slab", -1)
     from_below = from_behind(summed[:, 2 * width :], "slab", 1)
     force_sum = summed[:, width : 2 * width] + from_above + from_below

time: 437 us -> 479 us (1.096)
  waiting for transfers between devices: 111 us -> 135 us
  starting transfers between devices: 29.3 us -> 43.7 us
  other arithmetic: 113 us -> 118 us
    ppermute x0 -> x2, waiting for transfers between devices: none -> 83.5 us  [body(): lax.ppermute(summed, 'group', [(dev, dev ^ hop) for dev in range(4)])]
    psum x1 -> x0, waiting for transfers between devices: 59.9 us -> none  [body(): summed = lax.psum(partial_value, 'group')]
    all_to_all x1, starting transfers between devices: 13.2 us -> 20.5 us  [body(): lax.all_to_all(looked, 'slab', split_axis=0, concat_axis=0, tiled=True)]
    add x0 -> x2, other arithmetic: none -> 5.23 us  [body(): summed + lax.ppermute(summed, 'group', [(dev, dev ^ hop) for dev in range...]
  transfers between devices with their start and end apart: 8 -> 9, of which waited for: 6 -> 7; matrix products, arithmetic and copies ran while one was open for 1% -> 1% of each run, Pallas kernels for 0% -> 0%
where the time goes in v1:
time: 479 us; the launch traced here: 478 us
  local copies, waits for them, and re-layouts  141 us (29%)
  waiting for transfers between devices  135 us (28%)
  other arithmetic  118 us (25%)
  starting transfers between devices  43.7 us (9%)
  matrix products  18.6 us (4%)
  between operations  13.7 us (3%)
  blocking collectives  7.58 us (2%)
    ppermute x2, waiting for transfers between devices, body(): lax.ppermute(summed, 'group', [(dev, dev ^ hop) for dev in range(4)])  83.5 us
    scatter-add x1, other arithmetic, body(): jnp.zeros((3, 3 * width), jnp.float32).at[:, cell_nodes]  53.3 us
    scatter-add x1, other arithmetic, body(): jnp.zeros((3, width), jnp.float32).at[:, asked]  51.1 us
    psum x1, waiting for transfers between devices, body(): return disp_next + lax.psum(added, 'group')  38.1 us
    gather x2, local copies, waits for them, and re-layouts, body(): looked = jnp.moveaxis(jnp.take(disp_next, asked, axis=1), 0, 2)  36.4 us
    gather x2, local copies, waits for them, and re-layouts, body(): gathered = jnp.moveaxis(jnp.take(nearby, cell_nodes, axis=1), 0, 1)  34.5 us
    scatter-add x1, local copies, waits for them, and re-layouts, body(): jnp.zeros((3, 3 * width), jnp.float32).at[:, cell_nodes]  26.7 us
    all_to_all x1, starting transfers between devices, body(): lax.all_to_all(looked, 'slab', split_axis=0, concat_axis=0, tiled=True)  20.5 us
  transfers between devices with their start and end apart: 9, of which 7 were waited for; matrix products, arithmetic and copies ran while one was open for 1% of the time, Pallas kernels for 0%

profile of v1, /device:TPU:0, one launch (start us, length us, event | category | flops | bytes accessed | tf_op | source)
XLA Modules:
  0.0 478.1 jit_solution(6914125431201260819)
XLA Ops:
  7.8 2.4 collective-permute-start
  13.2 2.7 collective-permute-done.1
  17.2 15.8 %copy.143 = bf16[3,98304]{0,1:T(8,128)(2,1)} copy(bf16[3,98304]{1,0:T(4,128)(2,1)S(1)} %pad_maximum_fusion) | data formatting | bytes 1179648 | tf_op jit(solution)/shard_map/concatenate | solution.py:18
  33.0 32.5 %gather_fusion = bf16[6144,3]{1,0:T(8,128)(2,1)} fusion(bf16[3,98304]{0,1:T(8,128)(2,1)} %copy.143, s32[6144]{0:T(1024)S(1)} %broadcast_clamp_fusion.1), kind=kCustom, calls=%fused_computation | custom fusion | bytes 98304 | tf_op jit(solution)/shard_map/jit(_take)/gather | solution.py:82
  65.6 1.9 copy.144
  67.5 3.3 fusion.10
  71.2 4.1 convolution_bitcast_fusion
  75.2 2.2 copy.162
  77.5 53.3 %scatter_custom_fusion = f32[3,98304]{0,1:T(8,128)} fusion(s32[6144]{0:T(1024)S(1)} %reshape.1417, f32[6144,3]{1,0:T(8,128)} %bitcast.170, f32[]{:T(128)} %constant.16.clone.1), kind=kCustom, calls=%fused_computation.7 | custom fusion | flops 18432 | bytes 1180160 | tf_op jit(solution)/shard_map/scatter-add | solution.py:88
  130.7 26.7 %copy.150 = f32[3,98304]{1,0:T(4,128)} copy(f32[3,98304]{0,1:T(8,128)} %scatter_custom_fusion) | data formatting | bytes 2359296 | tf_op jit(solution)/shard_map/scatter-add | solution.py:88
  158.9 32.1 %collective-permute-done.2 = f32[3,98304]{1,0:T(4,128)S(1)} collective-permute-done((f32[3,98304]{1,0:T(4,128)}, f32[3,98304]{1,0:T(4,128)S(1)}, u32[]{:S(2)}, u32[]{:S(2)}) %collective-permute-start.2) | collective-permute-done | bytes 1179680 | tf_op jit(solution)/shard_map/ppermute | solution.py:92
  191.0 2.9 add.248
  194.0 2.6 collective-permute-start.3
  198.5 10.4 %all-to-all-start = ((s32[8,4,256]{2,1,0:T(4,128)}), s32[8,4,256]{2,1,0:T(4,128)S(1)}, u32[]{:S(2)}, u32[]{:S(2)}) async-start(s32[8,4,256]{2,1,0:T(4,128)} %reshape.1388), calls=%async_computation | async-start | bytes 65536 | tf_op jit(solution)/shard_map/all_to_all | solution.py:106
  208.9 4.8 %all-to-all-done = s32[8,4,256]{2,1,0:T(4,128)S(1)} async-done(((s32[8,4,256]{2,1,0:T(4,128)}), s32[8,4,256]{2,1,0:T(4,128)S(1)}, u32[]{:S(2)}, u32[]{:S(2)}) %all-to-all-start) | async-done | bytes 32800 | tf_op jit(solution)/shard_map/all_to_all | solution.py:106
  213.7 51.4 %collective-permute-done.3 = f32[3,98304]{1,0:T(4,128)} collective-permute-done((f32[3,98304]{1,0:T(4,128)}, f32[3,98304]{1,0:T(4,128)}, u32[]{:S(2)}, u32[]{:S(2)}) %collective-permute-start.3) | collective-permute-done | bytes 1179680 | tf_op jit(solution)/shard_map/ppermute | solution.py:92
  265.1 2.3 add.249
  268.9 3.5 collective-permute-start.5
  275.3 8.6 %copy.151 = f32[3,32768]{0,1:T(8,128)} copy(f32[3,32768]{1,0:T(4,128)S(1)} %fusion.7) | data formatting | bytes 786432 | tf_op jit(solution)/shard_map/sub | solution.py:96
  283.8 33.5 %gather_fusion.1 = f32[8192,3]{1,0:T(8,128)} fusion(f32[3,32768]{0,1:T(8,128)} %copy.151, s32[8192]{0:T(1024)S(1)} %broadcast_clamp_fusion), kind=kCustom, calls=%fused_computation.1 | custom fusion | bytes 229376 | tf_op jit(solution)/shard_map/jit(_take)/gather | solution.py:107
  317.3 2.8 copy.152
  320.9 20.5 %all-to-all-start.1 = ((f32[8,4,3,256]{3,1,2,0:T(4,128)}), f32[8,4,3,256]{3,1,2,0:T(4,128)S(1)}, u32[]{:S(2)}, u32[]{:S(2)}) async-start(f32[8,4,3,256]{3,1,2,0:T(4,128)} %select_bitcast_fusion), calls=%async_computation.1 | async-start | bytes 196608 | tf_op jit(solution)/shard_map/all_to_all | solution.py:108
  341.6 4.9 %all-to-all-done.1 = f32[8,4,3,256]{3,1,2,0:T(4,128)S(1)} async-done(((f32[8,4,3,256]{3,1,2,0:T(4,128)}), f32[8,4,3,256]{3,1,2,0:T(4,128)S(1)}, u32[]{:S(2)}, u32[]{:S(2)}) %all-to-all-start.1) | async-done | bytes 98336 | tf_op jit(solution)/shard_map/all_to_all | solution.py:108
  347.2 5.8 %fusion.4 = f32[32,3,128]{2,1,0:T(4,128)S(1)} fusion(f32[32,3,256]{2,1,0:T(4,128)S(1)} %gather_fusion.2, f32[32,128,256]{2,1,0:T(8,128)} %param.24, f32[32,3,128]{2,0,1:T(8,128)S(1)} %copy-done.4, f32[32,128]{1,0:T(8,128)S(1)} %convert_element_type.23), kind=kOutput, calls=%fused_computation.13 | convolution fusion | flops 37773312 | bytes 4407296 | tf_op jit(solution)/shard_map/bma,bia->bim/dot_general | solution.py:111
  353.1 3.4 fusion.23
  356.4 2.1 fusion.24
  360.1 7.6 %all_to_all.15 = f32[8,4,3,256]{3,1,2,0:T(4,128)S(1)} all-to-all(f32[8,4,3,256]{3,1,2,0:T(4,128)S(1)} %copy.156), channel_id=1, replica_groups=mesh['slab'=8,'group'=4] {'slab'}, dimensions={0} | all-to-all | bytes 196608 | tf_op jit(solution)/shard_map/all_to_all | solution.py:116
  367.7 2.6 copy.164
  370.3 51.1 %scatter_custom_fusion.3 = f32[3,32768]{0,1:T(8,128)} fusion(s32[8192]{0:T(1024)S(1)} %bitcast.176, f32[8192,3]{1,0:T(8,128)} %bitcast.169, f32[]{:T(128)} %constant.16.clone.1), kind=kCustom, calls=%fused_computation.9 | custom fusion | flops 24576 | bytes 393728 | tf_op jit(solution)/shard_map/scatter-add | solution.py:119
  421.3 9.8 %copy.159 = f32[3,32768]{1,0:T(4,128)} copy(f32[3,32768]{0,1:T(8,128)} %scatter_custom_fusion.3) | data formatting | bytes 786432 | tf_op jit(solution)/shard_map/scatter-add | solution.py:119
  431.2 38.1 %all-reduce.2.cloned.1.call-done = f32[3,32768]{1,0:T(4,128)} async-done(((f32[3,32768]{1,0:T(4,128)}), f32[3,32768]{1,0:T(4,128)}) %all-reduce.2.cloned.1.call-update) | async-done | bytes 393232 | tf_op jit(solution)/shard_map/psum | solution.py:120
  469.3 2.0 add.256
  (62 shorter events, 16.9 us)
Async XLA Ops:
  6.5 346.5 %copy-start = (f32[32,128,128]{2,1,0:T(8,128)S(1)}, f32[32,128,128]{2,1,0:T(8,128)}, u32[]{:S(2)}) copy-start(f32[32,128,128]{2,1,0:T(8,128)} %param.25) | copy-start | bytes 6291460
  7.8 5.4 %collective-permute-start = (bf16[3,32768]{1,0:T(4,128)(2,1)S(1)}, bf16[3,32768]{1,0:T(4,128)(2,1)S(1)}, u32[]{:S(2)}, u32[]{:S(2)}) collective-permute-start(bf16[3,32768]{1,0:T(4,128)(2,1)S(1)} %convert_element_type.19), channel_id=1, source_target_pairs={{0,4},{4,8},{8,12},{12,16},{16,20},{20,24},{24,28},{1,5},{5,9},{9,... | collective-permute-start | bytes 589832 | tf_op jit(solution)/shard_map/ppermute | solution.py:14
  10.2 5.6 %collective-permute-start.1 = (bf16[3,32768]{1,0:T(4,128)(2,1)S(1)}, bf16[3,32768]{1,0:T(4,128)(2,1)}, u32[]{:S(2)}, u32[]{:S(2)}) collective-permute-start(bf16[3,32768]{1,0:T(4,128)(2,1)S(1)} %convert_element_type.19), channel_id=1, source_target_pairs={{4,0},{8,4},{12,8},{16,12},{20,16},{24,20},{28,24},{5,1},{9,5},{13... | collective-permute-start | bytes 589832 | tf_op jit(solution)/shard_map/ppermute | solution.py:17
  33.0 37.8 %copy-start.7 = (f32[32]{0:T(128)S(1)}, f32[32]{0:T(128)}, u32[]{:S(2)}) copy-start(f32[32]{0:T(128)} %param.20) | copy-start | bytes 388
  33.0 37.8 %copy-start.9 = (f32[32]{0:T(128)S(1)}, f32[32]{0:T(128)}, u32[]{:S(2)}) copy-start(f32[32]{0:T(128)} %param.21) | copy-start | bytes 388
  33.0 38.1 %copy-start.6 = (f32[32,128]{1,0:T(8,128)S(1)}, f32[32,128]{1,0:T(8,128)}, u32[]{:S(2)}) copy-start(f32[32,128]{1,0:T(8,128)} %param.19) | copy-start | bytes 49156
  157.4 39.2 %copy-start.8 = (s32[32,1]{0,1:T(1,128)S(1)}, s32[32,1]{0,1:T(1,128)}, u32[]{:S(2)}) copy-start(s32[32,1]{0,1:T(1,128)} %param.22) | copy-start | bytes 388
  157.4 51.5 %copy-start.5 = (s32[32,128]{1,0:T(8,128)S(1)}, s32[32,128]{1,0:T(8,128)}, u32[]{:S(2)}) copy-start(s32[32,128]{1,0:T(8,128)} %param.27) | copy-start | bytes 49156
  157.4 33.7 %collective-permute-start.2 = (f32[3,98304]{1,0:T(4,128)}, f32[3,98304]{1,0:T(4,128)S(1)}, u32[]{:S(2)}, u32[]{:S(2)}) collective-permute-start(f32[3,98304]{1,0:T(4,128)} %copy.150), channel_id=1, source_target_pairs={{0,1},{1,0},{2,3},{3,2},{4,5},{5,4},{6,7},{7,6},{8,9},{9,8},{10,11... | collective-permute-start | bytes 3538952 | tf_op jit(solution)/shard_map/ppermute | solution.py:92
  194.0 79.9 %copy-start.2 = (f32[3,32768]{1,0:T(4,128)S(1)}, f32[3,32768]{1,0:T(4,128)}, u32[]{:S(2)}) copy-start(f32[3,32768]{1,0:T(4,128)} %param.14) | copy-start | bytes 1179652
  194.0 79.9 %copy-start.3 = (f32[32768]{0:T(1024)S(1)}, f32[32768]{0:T(1024)}, u32[]{:S(2)}) copy-start(f32[32768]{0:T(1024)} %param.16) | copy-start | bytes 393220
  194.0 71.1 %collective-permute-start.3 = (f32[3,98304]{1,0:T(4,128)}, f32[3,98304]{1,0:T(4,128)}, u32[]{:S(2)}, u32[]{:S(2)}) collective-permute-start(f32[3,98304]{1,0:T(4,128)} %add.248), channel_id=1, source_target_pairs={{0,2},{1,3},{2,0},{3,1},{4,6},{5,7},{6,4},{7,5},{8,10},{9,11},{10,... | collective-permute-start | bytes 3538952 | tf_op jit(solution)/shard_map/ppermute | solution.py:92
  198.5 15.2 %all-to-all-start = ((s32[8,4,256]{2,1,0:T(4,128)}), s32[8,4,256]{2,1,0:T(4,128)S(1)}, u32[]{:S(2)}, u32[]{:S(2)}) async-start(s32[8,4,256]{2,1,0:T(4,128)} %reshape.1388), calls=%async_computation | async-start | bytes 65536 | tf_op jit(solution)/shard_map/all_to_all | solution.py:106
  267.6 4.8 %collective-permute-start.4 = (f32[3,32768]{1,0:T(4,128)S(1)}, f32[3,32768]{1,0:T(4,128)S(1)}, u32[]{:S(2)}, u32[]{:S(2)}) collective-permute-start(f32[3,32768]{1,0:T(4,128)S(1)} %get-tuple-element.9), channel_id=1, source_target_pairs={{4,0},{8,4},{12,8},{16,12},{20,16},{24,20},{28,24},{5,1},{9,5},{13... | collective-permute-start | bytes 1179656 | tf_op jit(solution)/shard_map/ppermute | solution.py:25
  268.9 5.0 %collective-permute-start.5 = (f32[3,32768]{1,0:T(4,128)S(1)}, f32[3,32768]{1,0:T(4,128)S(1)}, u32[]{:S(2)}, u32[]{:S(2)}) collective-permute-start(f32[3,32768]{1,0:T(4,128)S(1)} %get-tuple-element.10), channel_id=1, source_target_pairs={{0,4},{4,8},{8,12},{12,16},{16,20},{20,24},{24,28},{1,5},{5,9},{9,... | collective-permute-start | bytes 1179656 | tf_op jit(solution)/shard_map/ppermute | solution.py:25
  283.8 63.4 %copy-start.4 = (f32[32,3,128]{2,0,1:T(8,128)S(1)}, f32[32,3,128]{2,0,1:T(8,128)}, u32[]{:S(2)}) copy-start(f32[32,3,128]{2,0,1:T(8,128)} %param.26) | copy-start | bytes 147460
  320.9 25.7 %all-to-all-start.1 = ((f32[8,4,3,256]{3,1,2,0:T(4,128)}), f32[8,4,3,256]{3,1,2,0:T(4,128)S(1)}, u32[]{:S(2)}, u32[]{:S(2)}) async-start(f32[8,4,3,256]{3,1,2,0:T(4,128)} %select_bitcast_fusion), calls=%async_computation.1 | async-start | bytes 196608 | tf_op jit(solution)/shard_map/all_to_all | solution.py:108
  341.3 127.9 %all-reduce.2.cloned.1.call-start = ((), (), s32[]{:S(2)}) async-start(), calls=%async_computation.3 | async-start | bytes 1048576 | tf_op jit(solution)/shard_map/psum | solution.py:120
  347.2 9.2 %copy-start.1 = (f32[32,128,256]{2,1,0:T(8,128)S(1)}, f32[32,128,256]{2,1,0:T(8,128)}, u32[]{:S(2)}) copy-start(f32[32,128,256]{2,1,0:T(8,128)} %param.24) | copy-start | bytes 12582916
Sparse Core Ops, SparseCore 0:
  431.3 37.8 all-reduce.1
